TPU v7x, 256 devices: a whole 4x4x8 slice. The times are simulated.
256 devices in a mesh: tm: 8 (over x, y_lo), space: 32 (over z, y_hi, core).
Axes of the slice: x: 4, y: 4 (y_hi: 2, y_lo: 2; y = y_hi * 2 + y_lo), z: 8, core: 2. Of those that a mesh axis runs over, the one named last changes fastest.
Arguments:
- iterate: float32 [64, 5, 65536], P('tm', None, 'space'), may hold values from -6 to 6
- right_side: float32 [64, 5, 65536], P('tm', None, 'space'), may hold values from -6 to 6
- jacobian: float32 [6, 5, 5, 65536], P(None, None, None, 'space'), may hold values from -0.24 to 0.24
- self_block: float32 [5, 5, 65536], P(None, None, 'space'), may hold values from -0.48 to 0.48
- cell_diag: float32 [5, 65536], P(None, 'space'), may hold values from 2.5 to 5
- neighbours: int32 [512, 6], P('space'), may hold values from 0 to 31, as said below
- face_list: int32 [256], P('space'), may hold values from 0 to 15, as said below
Outputs:
- updated: float32 [64, 5, 65536], P('tm', None, 'space')
- residual: float32 [64, 5, 65536], P('tm', None, 'space')
Inputs may be any that keep to these rules, and one draw needn't show every extreme that they name: `neighbours`: row b of slab s names 6 blocks in slab s's extended numbering: 0 to 15 its own blocks, 16 + h the h-th face block of slab s-1, 24 + h the h-th face block of slab s+1. Entry 0 always names a face block of the lower slab, entry 1 one of the upper slab, entries 2 to 5 own blocks. `face_list`: each slab's 8 entries are distinct local blocks of that slab; the last entry is always the slab's last block.
All inputs are finite; a program needn't handle non-finite values.
Results may differ from a plain program's by a relative error of at most 0.0001.
Values sent between devices are 32-bit elements; how exact they have to be, the bound alone decides.
A program may use at most 64 MiB of HBM per device.

v0:
```python
import functools

import jax
import jax.numpy as jnp
from jax import lax
from jax.experimental import pallas as pl
from jax.experimental.pallas import tpu as pltpu
from jax.sharding import PartitionSpec as P

NV = 5
BLK = 128
K = 6
BD = 16
H = 8
T = 8

WEIGHT = 0.5
COARSE = WEIGHT / 4.0
DAMP = 0.7
MESH = pl.DeviceIdType.MESH

FINE = ("f1", "f2", "f3", "f5", "f6")
SMALL = ("c0", "c1", "c2", "c3", "c4")
RING = ("f1", "f2", "f3", "f5", "f6", "c1", "c2", "c3", "c4")


def roll(x, n):
    return pltpu.roll(x, n % T, axis=0)


def kernel(n_tm, n_space, names, *refs):
    r = dict(zip(names, refs))
    tm = lax.axis_index("tm")
    slab = lax.axis_index("space")
    core = lax.rem(slab, 2)
    near_dev = (tm, slab + 1 - 2 * core)
    far_slab = slab - 1 + 2 * core
    has_far = jnp.logical_and(far_slab >= 0, far_slab < n_space)
    far_dev = (tm, far_slab)
    next_dev = (lax.rem(tm + 1, n_tm), slab)
    prev_dev = (lax.rem(tm + n_tm - 1, n_tm), slab)
    near_slot = 1 - core
    far_slot = core
    nb, fl = r["nb"], r["fl"]
    jac, sb, dg = r["jac"], r["sb"], r["dg"]
    v, pre, rhs = r["v"], r["pre"], r["rhs"]
    cf, cc = r["cf"], r["cc"]
    corr, cpre, cd = r["corr"], r["cpre"], r["cd"]

    sub = lax.broadcasted_iota(jnp.int32, (T, BLK), 0)
    sub4 = lax.rem(sub, 4)

    barrier = pltpu.get_barrier_semaphore()
    for dev in (near_dev, next_dev, prev_dev):
        pl.semaphore_signal(barrier, inc=1, device_id=dev, device_id_type=MESH)

    @pl.when(has_far)
    def _():
        pl.semaphore_signal(barrier, inc=1, device_id=far_dev, device_id_type=MESH)

    loads = {}
    for i, (src, dst) in enumerate(
        (("v_in", "v"), ("jac_in", "jac"), ("rhs_in", "rhs"), ("sb_in", "sb"), ("dg_in", "dg"))
    ):
        loads[dst] = pltpu.make_async_copy(r[src], r[dst], r["load_sem"].at[i])
        loads[dst].start()

    sem_index = {}
    for name in FINE + SMALL:
        for side in ("near", "far"):
            sem_index[name, side] = len(sem_index)
    for name in RING:
        sem_index[name, "ring"] = len(sem_index)

    def copy_of(name, side):
        i = sem_index[name, side]
        dev = {"near": near_dev, "far": far_dev, "ring": next_dev}[side]
        src = r["ring_out_" + name] if side == "ring" else r["face_out_" + name]
        return pltpu.make_async_remote_copy(
            src_ref=src,
            dst_ref=r[side + "_in_" + name],
            send_sem=r["send_sem"].at[i],
            recv_sem=r["recv_sem"].at[i],
            device_id=dev,
            device_id_type=MESH,
        )

    def send_faces(name):
        @pl.when(has_far)
        def _():
            copy_of(name, "far").start()

        copy_of(name, "near").start()

    def wait(name, side):
        if side == "far":

            @pl.when(has_far)
            def _():
                copy_of(name, side).wait_recv()

        else:
            copy_of(name, side).wait_recv()

    def row(ref, idx, k):
        return ref[idx + (pl.ds(k, T, stride=0), slice(None))]

    def own_block(b, x, g, field, three_w, timed):
        acc = []
        for a in range(NV):
            t = g[a] - (row(dg, (b,), a) + three_w) * x[a]
            t = t + timed(x[a])
            for j in range(NV):
                if j != a:
                    t = t - row(sb, (a, b), j) * x[j]
            acc.append(t)
        for k in range(2, K):
            at = nb[k, b]
            p = [field[j, at] for j in range(NV)]
            for a in range(NV):
                for j in range(NV):
                    acc[a] = acc[a] - row(jac, (a, j, b), k) * p[j]
        return acc

    def timed_fine(x):
        zero = jnp.zeros_like(x)
        one = jnp.where(sub >= 1, roll(x, 1), zero)
        two = jnp.where(sub >= 2, roll(x, 2), zero)
        return (4.0 * WEIGHT) * one - WEIGHT * two

    def timed_coarse(x):
        return (4.0 * COARSE) * jnp.where(sub >= 4, roll(x, 4), jnp.zeros_like(x))

    def blocks(body):
        def step(b, carry):
            body(b)
            return carry

        lax.fori_loop(0, BD, step, 0)

    def own(field, g, out, three_w, timed):
        def body(b):
            x = [field[j, b] for j in range(NV)]
            acc = own_block(b, x, [g[a, b] for a in range(NV)], field, three_w, timed)
            for a in range(NV):
                out[a, b] = acc[a]

        blocks(body)

    def rim(acc, b, field, slot):
        at = jnp.bitwise_and(nb[slot, b], H - 1)
        p = [field[j, at] for j in range(NV)]
        for a in range(NV):
            for j in range(NV):
                acc[a] = acc[a] - row(jac, (a, j, b), slot) * p[j]
        return acc

    def fold_rim(out, field, slot):
        def body(b):
            acc = rim([out[a, b] for a in range(NV)], b, field, slot)
            for a in range(NV):
                out[a, b] = acc[a]

        blocks(body)

    def pack_ring(name, rows_of, place):
        out = r["ring_out_" + name]

        def body(g, carry):
            for a in range(NV):
                tile = None
                for i in range(4):
                    piece = place(rows_of(a, 4 * g + i), i)
                    tile = piece if tile is None else jnp.where(group_of(i), piece, tile)
                out[a, g] = tile
            return carry

        group_of = (lambda i: sub // 2 == i) if place is place_fine else (lambda i: sub4 == i)
        lax.fori_loop(0, BD // 4, body, 0)
        copy_of(name, "ring").start()

    def place_fine(x, i):
        q = WEIGHT * (roll(x, 2) - jnp.where(sub == 0, 4.0 * roll(x, 1), jnp.zeros_like(x)))
        return roll(q, 2 * i) if i else q

    def place_coarse(x, i):
        other = roll(x, 4)
        return COARSE * jnp.where(sub >= 4, x, x - 4.0 * other)

    def fold_ring_fine(name, out):
        src = r["ring_in_" + name]

        def body(g, carry):
            for a in range(NV):
                tile = src[a, g]
                for i in range(4):
                    q = roll(tile, T - 2 * i) if i else tile
                    out[a, 4 * g + i] = out[a, 4 * g + i] - jnp.where(sub < 2, q, jnp.zeros_like(q))
            return carry

        lax.fori_loop(0, BD // 4, body, 0)

    def spread(tile, turns, i):
        x = None
        for u in range(4):
            y = turns[u - i]
            x = y if x is None else jnp.where(sub4 == u, y, x)
        return x

    def turns_of(tile):
        return {d: (roll(tile, d) if d else tile) for d in range(-3, 4)}

    def fold_ring_coarse(name, out):
        src = r["ring_in_" + name]

        def body(g, carry):
            for a in range(NV):
                tile = src[a, g]
                turns = turns_of(tile)
                for i in range(4):
                    out[a, 4 * g + i] = out[a, 4 * g + i] - spread(tile, turns, i)
            return carry

        lax.fori_loop(0, BD // 4, body, 0)

    def unpack(name, side):
        src, out = r[side + "_in_" + name], r["rim_" + side]

        def body(a, carry):
            for g in range(H // 4):
                tile = src[a, g]
                turns = turns_of(tile)
                for i in range(4):
                    out[a, 4 * g + i] = spread(tile, turns, i)
            return carry

        lax.fori_loop(0, NV, body, 0)
        return out

    def mean4(x):
        x = x + jnp.where(lax.rem(sub, 2) == 0, roll(x, -1), roll(x, 1))
        x = x + jnp.where(sub4 < 2, roll(x, -2), roll(x, 2))
        return 0.25 * x

    def pack_faces(name, value_of):
        out = r["face_out_" + name]

        def body(g, carry):
            got = [value_of(4 * g + i) for i in range(4)]
            for a in range(NV):
                tile = got[0][a]
                for i in range(1, 4):
                    tile = jnp.where(sub4 == i, got[i][a], tile)
                out[a, g] = tile
            return carry

        lax.fori_loop(0, H // 4, body, 0)
        send_faces(name)

    def full_faces(name, value_of):
        out = r["face_out_" + name]

        def body(h, carry):
            got = value_of(h)
            for a in range(NV):
                out[a, h] = got[a]
            return carry

        lax.fori_loop(0, H, body, 0)
        send_faces(name)

    def swept(b, field, p, scale, far):
        acc = rim([p[a, b] for a in range(NV)], b, far, far_slot)
        return [field[a, b] + scale[a, b] * acc[a] for a in range(NV)]

    def store(ref, b, values):
        for a in range(NV):
            ref[a, b] = values[a]

    @pl.when(jnp.logical_not(has_far))
    def _():
        for name in FINE + SMALL:
            ref = r["far_in_" + name]

            def clear(a, carry, ref=ref):
                for i in range(ref.shape[1]):
                    ref[a, i] = jnp.zeros((T, BLK), jnp.float32)
                return carry

            lax.fori_loop(0, NV, clear, 0)

    loads["v"].wait()
    n_near = jnp.where(has_far, 4, 3)
    pl.semaphore_wait(barrier, n_near)
    full_faces("f1", lambda h: [v[a, fl[h]] for a in range(NV)])
    pack_ring("f1", lambda a, b: v[a, b], place_fine)

    for name in ("jac", "rhs", "sb", "dg"):
        loads[name].wait()

    def scales(b):
        for a in range(NV):
            d = row(dg, (b,), a)
            cf[a, b] = DAMP / (3.0 * WEIGHT + d)
            cc[a, b] = DAMP / (3.0 * COARSE + d)

    blocks(scales)

    def settle(name, out):
        wait(name, "near")
        fold_rim(out, r["near_in_" + name], near_slot)
        wait(name, "ring")
        fold_ring_fine(name, out)
        wait(name, "far")

    own(v, rhs, pre, 3.0 * WEIGHT, timed_fine)
    settle("f1", pre)
    far = r["far_in_f1"]
    full_faces("f2", lambda h, far=far: swept(fl[h], v, pre, cf, far))
    blocks(lambda b, far=far: store(v, b, swept(b, v, pre, cf, far)))
    pack_ring("f2", lambda a, b: v[a, b], place_fine)
    own(v, rhs, pre, 3.0 * WEIGHT, timed_fine)
    settle("f2", pre)
    far = r["far_in_f2"]
    pack_faces("c0", lambda h, far=far: [mean4(x) for x in swept(fl[h], v, pre, cf, far)])
    blocks(lambda b, far=far: store(v, b, swept(b, v, pre, cf, far)))
    pack_ring("f3", lambda a, b: v[a, b], place_fine)
    full_faces("f3", lambda h: [v[a, fl[h]] for a in range(NV)])

    own(v, rhs, pre, 3.0 * WEIGHT, timed_fine)
    wait("f3", "ring")
    fold_ring_fine("f3", pre)
    blocks(lambda b: store(cpre, b, [mean4(pre[a, b]) for a in range(NV)]))
    wait("c0", "near")
    fold_rim(cpre, unpack("c0", "near"), near_slot)
    wait("c0", "far")
    far = unpack("c0", "far")

    def first(b):
        acc = rim([cpre[a, b] for a in range(NV)], b, far, far_slot)
        return acc, [cc[a, b] * acc[a] for a in range(NV)]

    def first_store(b):
        acc, values = first(b)
        store(cd, b, acc)
        store(corr, b, values)

    pack_faces("c1", lambda h: first(fl[h])[1])
    blocks(first_store)
    pack_ring("c1", lambda a, b: corr[a, b], place_coarse)

    for name, later in (("c1", "c2"), ("c2", "c3"), ("c3", "c4")):
        own(corr, cd, cpre, 3.0 * COARSE, timed_coarse)
        wait(name, "near")
        fold_rim(cpre, unpack(name, "near"), near_slot)
        wait(name, "ring")
        fold_ring_coarse(name, cpre)
        if name == "c2":
            wait("f3", "near")
            fold_rim(pre, r["near_in_f3"], near_slot)
            wait("f3", "far")
            fold_rim(pre, r["far_in_f3"], far_slot)
        wait(name, "far")
        far = unpack(name, "far")
        pack_faces(later, lambda h, far=far: swept(fl[h], corr, cpre, cc, far))
        blocks(lambda b, far=far: store(corr, b, swept(b, corr, cpre, cc, far)))
        pack_ring(later, lambda a, b: corr[a, b], place_fine if later == "c4" else place_coarse)

    def correct(b):
        for a in range(NV):
            v[a, b] = v[a, b] + corr[a, b]

    own(corr, pre, pre, 3.0 * WEIGHT, timed_fine)
    blocks(correct)
    wait("c4", "near")
    fold_rim(pre, unpack("c4", "near"), near_slot)
    wait("c4", "ring")
    fold_ring_fine("c4", pre)
    wait("c4", "far")
    far = unpack("c4", "far")
    full_faces("f5", lambda h, far=far: swept(fl[h], v, pre, cf, far))
    blocks(lambda b, far=far: store(v, b, swept(b, v, pre, cf, far)))
    pack_ring("f5", lambda a, b: v[a, b], place_fine)
    own(v, rhs, pre, 3.0 * WEIGHT, timed_fine)
    settle("f5", pre)
    far = r["far_in_f5"]
    full_faces("f6", lambda h, far=far: swept(fl[h], v, pre, cf, far))
    blocks(lambda b, far=far: store(v, b, swept(b, v, pre, cf, far)))
    pack_ring("f6", lambda a, b: v[a, b], place_fine)
    save_v = pltpu.make_async_copy(v, r["v_out"], r["load_sem"].at[5])
    save_v.start()
    own(v, rhs, pre, 3.0 * WEIGHT, timed_fine)
    settle("f6", pre)
    fold_rim(pre, r["far_in_f6"], far_slot)
    save_r = pltpu.make_async_copy(pre, r["r_out"], r["load_sem"].at[6])
    save_r.start()
    for name, side in sem_index:
        if side == "far":

            @pl.when(has_far)
            def _(name=name, side=side):
                copy_of(name, side).wait_send()

        else:
            copy_of(name, side).wait_send()
    save_v.wait()
    save_r.wait()


def body(n_tm, n_space, iterate, right_side, jacobian, self_block, cell_diag, neighbours, face_list):
    def tiles(x):
        return x.reshape(T, NV, BD, BLK).transpose(1, 2, 0, 3)

    def untile(x):
        return x.transpose(2, 0, 1, 3).reshape(T, NV, BD * BLK)

    args = {
        "nb": neighbours.T,
        "fl": face_list,
        "v_in": tiles(iterate),
        "jac_in": jacobian.reshape(K, NV, NV, BD, BLK).transpose(1, 2, 3, 0, 4),
        "rhs_in": tiles(right_side),
        "sb_in": self_block.reshape(NV, NV, BD, BLK).transpose(0, 2, 1, 3),
        "dg_in": cell_diag.reshape(NV, BD, BLK).transpose(1, 0, 2),
    }
    field = (NV, BD, T, BLK)
    face = (NV, H, T, BLK)
    small = (NV, H // 4, T, BLK)
    ring = (NV, BD // 4, T, BLK)
    scratch = {
        "v": field,
        "jac": (NV, NV, BD, K, BLK),
        "rhs": field,
        "sb": (NV, BD, NV, BLK),
        "dg": (BD, NV, BLK),
        "pre": field,
        "cf": field,
        "cc": field,
        "corr": field,
        "cpre": field,
        "cd": field,
        "rim_near": face,
        "rim_far": face,
    }
    for name in FINE + SMALL:
        for key in ("face_out_", "near_in_", "far_in_"):
            scratch[key + name] = face if name in FINE else small
    for name in RING:
        for key in ("ring_out_", "ring_in_"):
            scratch[key + name] = ring
    n_sems = 2 * len(FINE + SMALL) + len(RING)
    names = list(args) + ["v_out", "r_out"] + list(scratch) + ["load_sem", "send_sem", "recv_sem"]
    hbm = pl.BlockSpec(memory_space=pltpu.HBM)
    smem = pl.BlockSpec(memory_space=pltpu.SMEM)
    out = pl.pallas_call(
        functools.partial(kernel, n_tm, n_space, names),
        out_shape=(jax.ShapeDtypeStruct(field, jnp.float32),) * 2,
        in_specs=[smem, smem] + [hbm] * 5,
        out_specs=(hbm, hbm),
        scratch_shapes=[pltpu.VMEM(shape, jnp.float32) for shape in scratch.values()]
        + [
            pltpu.SemaphoreType.DMA((7,)),
            pltpu.SemaphoreType.DMA((n_sems,)),
            pltpu.SemaphoreType.DMA((n_sems,)),
        ],
        compiler_params=pltpu.CompilerParams(
            collective_id=0, has_side_effects=True, vmem_limit_bytes=48 * 1024 * 1024
        ),
        name="vcycle",
    )(*args.values())
    return tuple(untile(x) for x in out)


def solution(mesh):
    in_specs = (
        P("tm", None, "space"),
        P("tm", None, "space"),
        P(None, None, None, "space"),
        P(None, None, "space"),
        P(None, "space"),
        P("space", None),
        P("space"),
    )
    out_specs = (P("tm", None, "space"), P("tm", None, "space"))
    step = functools.partial(body, mesh.shape["tm"], mesh.shape["space"])
    return jax.shard_map(step, mesh=mesh, in_specs=in_specs, out_specs=out_specs, check_vma=False)
```

profile of v0, /device:TPU:73, one launch (start us, length us, event | category | flops | bytes accessed | tf_op | source)
XLA Modules:
  0.0 74.7 jit_solution(16294670422937428898)
XLA Ops:
  0.6 0.0 copy-start
  0.6 1.4 %copy-done = f32[6,5,5,2048]{3,0,2,1:T(8,128)S(1)} copy-done((f32[6,5,5,2048]{3,0,2,1:T(8,128)S(1)}, f32[6,5,5,2048]{3,0,2,1:T(8,128)}, u32[]{:S(2)}) %copy-start) | copy-done | bytes 1228824
  2.1 0.0 copy-start.1
  2.1 1.0 %copy-done.1 = f32[8,5,2048]{2,0,1:T(8,128)S(1)} copy-done((f32[8,5,2048]{2,0,1:T(8,128)S(1)}, f32[8,5,2048]{2,0,1:T(8,128)}, u32[]{:S(2)}) %copy-start.1) | copy-done | bytes 327704
  3.0 0.0 copy-start.2
  3.0 1.0 %copy-done.2 = f32[8,5,2048]{2,0,1:T(8,128)S(1)} copy-done((f32[8,5,2048]{2,0,1:T(8,128)S(1)}, f32[8,5,2048]{2,0,1:T(8,128)}, u32[]{:S(2)}) %copy-start.2) | copy-done | bytes 327704
  4.0 0.0 copy-start.3
  4.0 1.0 %copy-done.3 = f32[5,5,2048]{2,1,0:T(8,128)S(1)} copy-done((f32[5,5,2048]{2,1,0:T(8,128)S(1)}, f32[5,5,2048]{2,1,0:T(8,128)}, u32[]{:S(2)}) %copy-start.3) | copy-done | bytes 204824
  5.0 0.0 copy-start.4
  5.0 0.8 %copy-done.4 = f32[5,2048]{1,0:T(8,128)S(1)} copy-done((f32[5,2048]{1,0:T(8,128)S(1)}, f32[5,2048]{1,0:T(8,128)}, u32[]{:S(2)}) %copy-start.4) | copy-done | bytes 40984
  5.8 0.0 copy-start.5
  5.8 0.7 copy-done.5
  6.5 0.0 copy-start.6
  6.5 0.7 copy-done.6
  7.2 66.1 %vcycle.1 = (f32[5,16,8,128]{3,2,1,0:T(8,128)S(1)}, f32[5,16,8,128]{3,2,1,0:T(8,128)S(1)}) custom-call(s32[6,16]{1,0:T(8,128)S(1)} %bitcast.29, s32[8]{0:T(128)S(1)} %copy-done.6, f32[5,16,8,128]{3,2,1,0:T(8,128)S(1)} %bitcast.23, f32[5,5,16,6,128]{4,3,2,1,0:T(8,128)S(1)} %bitcast.22, f32[5,16,8,128]{3,2,1,0:T(8,128)S(1)} %bitcast.24, ...), custom_call_target="tpu_custom_call" | custom-call | tf_op jit(solution)/shard_map/vcycle/pallas_call | solution.py:455
  73.2 0.7 copy.11
  74.0 0.7 copy.12
Async XLA Ops:
  0.6 1.4 %copy-start = (f32[6,5,5,2048]{3,0,2,1:T(8,128)S(1)}, f32[6,5,5,2048]{3,0,2,1:T(8,128)}, u32[]{:S(2)}) copy-start(f32[6,5,5,2048]{3,0,2,1:T(8,128)} %param.9) | copy-start | bytes 3686404
  2.1 1.0 %copy-start.1 = (f32[8,5,2048]{2,0,1:T(8,128)S(1)}, f32[8,5,2048]{2,0,1:T(8,128)}, u32[]{:S(2)}) copy-start(f32[8,5,2048]{2,0,1:T(8,128)} %param.7) | copy-start | bytes 983044
  3.0 1.0 %copy-start.2 = (f32[8,5,2048]{2,0,1:T(8,128)S(1)}, f32[8,5,2048]{2,0,1:T(8,128)}, u32[]{:S(2)}) copy-start(f32[8,5,2048]{2,0,1:T(8,128)} %param.8) | copy-start | bytes 983044
  4.0 1.0 %copy-start.3 = (f32[5,5,2048]{2,1,0:T(8,128)S(1)}, f32[5,5,2048]{2,1,0:T(8,128)}, u32[]{:S(2)}) copy-start(f32[5,5,2048]{2,1,0:T(8,128)} %param.10) | copy-start | bytes 614404
  5.0 0.8 %copy-start.4 = (f32[5,2048]{1,0:T(8,128)S(1)}, f32[5,2048]{1,0:T(8,128)}, u32[]{:S(2)}) copy-start(f32[5,2048]{1,0:T(8,128)} %param.11) | copy-start | bytes 122884
  5.8 0.7 copy-start.5
  6.5 0.7 copy-start.6
where the time goes:
time: 75 us; the launch traced here: 74.7 us
  Pallas kernels  66.1 us (88%)
  local copies, waits for them, and re-layouts  7.97 us (11%)
    pallas_call x1, Pallas kernels, body(): pl.pallas_call(functools.partial(kernel, n_tm, n_space, names), out_shape...  66.1 us
    unnamed x16, local copies, waits for them, and re-layouts  7.97 us

commit v1 on v0

v1 whole, which is shorter than its diff:
```python
import functools

import jax
import jax.numpy as jnp
from jax import lax
from jax.experimental import pallas as pl
from jax.experimental.pallas import tpu as pltpu
from jax.sharding import PartitionSpec as P

NV = 5
BLK = 128
K = 6
BD = 16
H = 8
T = 8

WEIGHT = 0.5
COARSE = WEIGHT / 4.0
DAMP = 0.7
MESH = pl.DeviceIdType.MESH

FINE = ("f1", "f2", "f3", "f5", "f6")
SMALL = ("c0", "c1", "c2", "c3", "c4")
PARTS = ((0, 2), (2, 2), (4, 1))
RING = ("f1", "f2", "f3", "f5", "f6", "c1", "c2", "c3", "c4")


def roll(x, n):
    return pltpu.roll(x, n % T, axis=0)


def kernel(n_tm, n_space, names, *refs):
    r = dict(zip(names, refs))
    tm = lax.axis_index("tm")
    slab = lax.axis_index("space")
    core = lax.rem(slab, 2)
    near_dev = (tm, slab + 1 - 2 * core)
    far_slab = slab - 1 + 2 * core
    has_far = jnp.logical_and(far_slab >= 0, far_slab < n_space)
    far_dev = (tm, far_slab)
    next_dev = (lax.rem(tm + 1, n_tm), slab)
    prev_dev = (lax.rem(tm + n_tm - 1, n_tm), slab)
    near_slot = 1 - core
    far_slot = core
    nb, fl = r["nb"], r["fl"]
    jac, sb, dg = r["jac"], r["sb"], r["dg"]
    v, pre, rhs = r["v"], r["pre"], r["rhs"]
    cf, cc = r["cf"], r["cc"]
    corr, cpre, cd = r["corr"], r["cpre"], r["cd"]
    late, rank, others = r["late"], r["rank"], r["others"]

    sub = lax.broadcasted_iota(jnp.int32, (T, BLK), 0)
    sub4 = lax.rem(sub, 4)

    barrier = pltpu.get_barrier_semaphore()
    for dev in (near_dev, next_dev, prev_dev):
        pl.semaphore_signal(barrier, inc=1, device_id=dev, device_id_type=MESH)

    @pl.when(has_far)
    def _():
        pl.semaphore_signal(barrier, inc=1, device_id=far_dev, device_id_type=MESH)

    loads = {}
    for i, (src, dst) in enumerate(
        (
            ("fl_in", "fl"),
            ("v_in", "v"),
            ("nb_in", "nb"),
            ("jac_in", "jac"),
            ("rhs_in", "rhs"),
            ("sb_in", "sb"),
            ("dg_in", "dg"),
        )
    ):
        loads[dst] = pltpu.make_async_copy(r[src], r[dst], r["load_sem"].at[i])
        loads[dst].start()

    sem_index = {}
    for name in FINE + SMALL:
        for side in ("near", "far"):
            for part in PARTS if (name, side) == ("f3", "far") else (None,):
                sem_index[name, side, part] = len(sem_index)
    for name in RING:
        for side in ("ring0", "ring1"):
            sem_index[name, side, None] = len(sem_index)

    def copy_of(name, side, part=None):
        i = sem_index[name, side, part]
        if side in ("near", "far"):
            src, dst = r["face_out_" + name], r[side + "_in_" + name]
            dev = near_dev if side == "near" else far_dev
            if part:
                src, dst = src.at[pl.ds(*part)], dst.at[pl.ds(*part)]
        else:
            src, dst = (r["ring_%s_%s_%s" % (way, name, side[-1])] for way in ("out", "in"))
            dev = next_dev
        return pltpu.make_async_remote_copy(
            src_ref=src,
            dst_ref=dst,
            send_sem=r["send_sem"].at[i],
            recv_sem=r["recv_sem"].at[i],
            device_id=dev,
            device_id_type=MESH,
        )

    def send_far(name, part=None):
        @pl.when(has_far)
        def _():
            copy_of(name, "far", part).start()

    def send_faces(name):
        send_far(name)
        copy_of(name, "near").start()

    def wait(name, side):
        if side == "far":

            @pl.when(has_far)
            def _():
                for part in PARTS if name == "f3" else (None,):
                    copy_of(name, side, part).wait_recv()

        else:
            copy_of(name, side).wait_recv()

    def row(ref, idx, k):
        return ref[idx + (pl.ds(k, T, stride=0), slice(None))]

    def own_block(b, x, g, field, three_w, timed):
        acc = []
        for a in range(NV):
            t = g[a] - (row(dg, (b,), a) + three_w) * x[a]
            t = t + timed(x[a])
            for j in range(NV):
                if j != a:
                    t = t - row(sb, (a, b), j) * x[j]
            acc.append(t)
        for k in range(2, K):
            at = nb[k, b]
            p = [field[j, at] for j in range(NV)]
            for a in range(NV):
                for j in range(NV):
                    acc[a] = acc[a] - row(jac, (a, j, b), k) * p[j]
        return acc

    def timed_fine(x):
        zero = jnp.zeros_like(x)
        one = jnp.where(sub >= 1, roll(x, 1), zero)
        two = jnp.where(sub >= 2, roll(x, 2), zero)
        return (4.0 * WEIGHT) * one - WEIGHT * two

    def timed_coarse(x):
        return (4.0 * COARSE) * jnp.where(sub >= 4, roll(x, 4), jnp.zeros_like(x))

    def grouped(count, values_of, keep, width):
        def step(g, carry):
            at = [width * g + i for i in range(width)]
            got = [values_of(b) for b in at]
            for b, values in zip(at, got):
                keep(b, values)
            return carry

        lax.fori_loop(0, count // width, step, 0)

    def store(ref, b, values):
        for a in range(NV):
            ref[a, b] = values[a]

    def own(field, g, out, three_w, timed):
        def values_of(b):
            x = [field[j, b] for j in range(NV)]
            return own_block(b, x, [g[a, b] for a in range(NV)], field, three_w, timed)

        grouped(BD, values_of, functools.partial(store, out), 2)

    def rim(acc, b, field, slot):
        at = jnp.bitwise_and(nb[slot, b], H - 1)
        p = [field[j, at] for j in range(NV)]
        for a in range(NV):
            for j in range(NV):
                acc[a] = acc[a] - row(jac, (a, j, b), slot) * p[j]
        return acc

    def fold_rim(out, field, slot):
        def values_of(b):
            return rim([out[a, b] for a in range(NV)], b, field, slot)

        grouped(BD, values_of, functools.partial(store, out), 4)

    def place_fine(x, i):
        q = WEIGHT * (roll(x, 2) - jnp.where(sub == 0, 4.0 * roll(x, 1), jnp.zeros_like(x)))
        return roll(q, 2 * i) if i else q

    def place_coarse(x, i):
        return COARSE * jnp.where(sub >= 4, x, x - 4.0 * roll(x, 4))

    def ring_tile(four, place):
        tile = place(four[0], 0)
        for i in range(1, 4):
            mine = lax.div(sub, 2) == i if place is place_fine else sub4 == i
            tile = jnp.where(mine, place(four[i], i), tile)
        return tile

    def send_others(name, field, place):
        out = r["ring_out_" + name + "_1"]
        for g in range(2):
            got = [[field[a, others[4 * g + i]] for i in range(4)] for a in range(NV)]
            for a in range(NV):
                out[a, g] = ring_tile(got[a], place)
        copy_of(name, "ring1").start()

    def spread(turns, i):
        x = turns[-i]
        for u in range(1, 4):
            x = jnp.where(sub4 == u, turns[u - i], x)
        return x

    def turns_of(tile):
        return {d: (roll(tile, d) if d else tile) for d in range(-3, 4)}

    def open_ring(name, part, fine):
        wait(name, "ring%d" % part)
        src = r["ring_in_%s_%d" % (name, part)]

        def body(a, carry):
            got = []
            for g in range(2):
                tile = src[a, g]
                turns = None if fine else turns_of(tile)
                for i in range(4):
                    if fine:
                        q = roll(tile, T - 2 * i) if i else tile
                        got.append(jnp.where(sub < 2, q, jnp.zeros_like(q)))
                    else:
                        got.append(spread(turns, i))
            for i in range(H):
                late[a, H * part + i] = got[i]
            return carry

        lax.fori_loop(0, NV, body, 0)

    def unpack(name, side):
        wait(name, side)
        src, out = r[side + "_in_" + name], r["rim_" + side]

        def body(a, carry):
            got = []
            for g in range(H // 4):
                turns = turns_of(src[a, g])
                got += [spread(turns, i) for i in range(4)]
            for i in range(H):
                out[a, i] = got[i]
            return carry

        lax.fori_loop(0, NV, body, 0)
        return out

    def mean4(x):
        x = x + jnp.where(lax.rem(sub, 2) == 0, roll(x, -1), roll(x, 1))
        x = x + jnp.where(sub4 < 2, roll(x, -2), roll(x, 2))
        return 0.25 * x

    def faces(value_of, place, ring_name, full=None, small=None, average=False):
        kept = r["face_out_" + full] if full else r["face_kept"]
        for g in range(2):
            got = [value_of(4 * g + i) for i in range(4)]
            for a in range(NV):
                for i in range(4):
                    kept[a, 4 * g + i] = got[i][a]
                if small:
                    four = [mean4(x[a]) if average else x[a] for x in got]
                    tile = four[0]
                    for i in range(1, 4):
                        tile = jnp.where(sub4 == i, four[i], tile)
                    r["face_out_" + small][a, g] = tile
        send_faces(small or full)
        for g in range(2):
            for a in range(NV):
                four = [kept[a, 4 * g + i] for i in range(4)]
                r["ring_out_" + ring_name + "_0"][a, g] = ring_tile(four, place)
        copy_of(ring_name, "ring0").start()

    def swept_face(field, p, scale, far, h):
        b = fl[h]
        acc = rim([p[a, b] - late[a, h] for a in range(NV)], b, far, far_slot)
        return [field[a, b] + scale[a, b] * acc[a] for a in range(NV)]

    def swept(field, p, scale, far, b):
        at = rank[b]
        acc = rim([p[a, b] - late[a, at] for a in range(NV)], b, far, far_slot)
        return [field[a, b] + scale[a, b] * acc[a] for a in range(NV)]

    def sweep(field, p, scale, far):
        grouped(BD, functools.partial(swept, field, p, scale, far), functools.partial(store, field), 4)

    @pl.when(jnp.logical_not(has_far))
    def _():
        for name in FINE + SMALL:
            ref = r["far_in_" + name]

            def clear(a, carry, ref=ref):
                for i in range(ref.shape[1]):
                    ref[a, i] = jnp.zeros((T, BLK), jnp.float32)
                return carry

            lax.fori_loop(0, NV, clear, 0)

    loads["fl"].wait()
    loads["v"].wait()
    pl.semaphore_wait(barrier, jnp.where(has_far, 4, 3))
    faces(lambda h: [v[a, fl[h]] for a in range(NV)], place_fine, "f1", full="f1")

    def rank_of(b, count):
        at = jnp.minimum(H + count, BD - 1)
        for h in range(H):
            at = jnp.where(fl[h] == b, h, at)
        rank[b] = at
        return jnp.where(at >= H, count + 1, count)

    lax.fori_loop(0, BD, rank_of, jnp.int32(0))

    def other_of(i, carry):
        b = jnp.int32(0)
        for c in range(BD):
            b = jnp.where(rank[c] == H + i, c, b)
        others[i] = b
        return carry

    lax.fori_loop(0, H, other_of, 0)
    send_others("f1", v, place_fine)
    for name in ("nb", "jac", "rhs", "sb", "dg"):
        loads[name].wait()

    def scales(b):
        d = [row(dg, (b,), a) for a in range(NV)]
        return [DAMP / (3.0 * WEIGHT + x) for x in d] + [DAMP / (3.0 * COARSE + x) for x in d]

    def keep_scales(b, values):
        store(cf, b, values[:NV])
        store(cc, b, values[NV:])

    grouped(BD, scales, keep_scales, 2)

    def arrive(name, out):
        wait(name, "near")
        fold_rim(out, r["near_in_" + name], near_slot)
        open_ring(name, 0, True)
        wait(name, "far")
        return r["far_in_" + name]

    own(v, rhs, pre, 3.0 * WEIGHT, timed_fine)
    far = arrive("f1", pre)
    faces(functools.partial(swept_face, v, pre, cf, far), place_fine, "f2", full="f2")
    open_ring("f1", 1, True)
    sweep(v, pre, cf, far)
    send_others("f2", v, place_fine)
    own(v, rhs, pre, 3.0 * WEIGHT, timed_fine)
    far = arrive("f2", pre)
    faces(functools.partial(swept_face, v, pre, cf, far), place_fine, "f3", full="f3", small="c0", average=True)
    open_ring("f2", 1, True)
    sweep(v, pre, cf, far)
    send_others("f3", v, place_fine)
    send_far("f3", PARTS[0])
    copy_of("f3", "near").start()

    own(v, rhs, pre, 3.0 * WEIGHT, timed_fine)
    grouped(BD, lambda b: [mean4(pre[a, b]) for a in range(NV)], functools.partial(store, cpre), 2)
    fold_rim(cpre, unpack("c0", "near"), near_slot)
    open_ring("f3", 0, True)
    far = unpack("c0", "far")

    def first_face(h):
        b = fl[h]
        acc = rim([cpre[a, b] - mean4(late[a, h]) for a in range(NV)], b, far, far_slot)
        return [cc[a, b] * acc[a] for a in range(NV)]

    def first(b):
        q = [late[a, rank[b]] for a in range(NV)]
        acc = rim([cpre[a, b] - mean4(q[a]) for a in range(NV)], b, far, far_slot)
        return acc + [cc[a, b] * acc[a] for a in range(NV)] + [pre[a, b] - q[a] for a in range(NV)]

    def keep_first(b, values):
        store(cd, b, values[:NV])
        store(corr, b, values[NV : 2 * NV])
        store(pre, b, values[2 * NV :])

    faces(first_face, place_coarse, "c1", small="c1")
    open_ring("f3", 1, True)
    grouped(BD, first, keep_first, 2)
    send_others("c1", corr, place_coarse)
    send_far("f3", PARTS[1])

    for name, later in (("c1", "c2"), ("c2", "c3"), ("c3", "c4")):
        place = place_fine if later == "c4" else place_coarse
        own(corr, cd, cpre, 3.0 * COARSE, timed_coarse)
        fold_rim(cpre, unpack(name, "near"), near_slot)
        open_ring(name, 0, False)
        if name == "c3":
            for side, slot in (("near", near_slot), ("far", far_slot)):
                wait("f3", side)
                fold_rim(pre, r[side + "_in_f3"], slot)
        far = unpack(name, "far")
        faces(functools.partial(swept_face, corr, cpre, cc, far), place, later, small=later)
        open_ring(name, 1, False)
        sweep(corr, cpre, cc, far)
        send_others(later, corr, place)
        if later == "c2":
            send_far("f3", PARTS[2])

    own(corr, pre, pre, 3.0 * WEIGHT, timed_fine)
    grouped(BD, lambda b: [v[a, b] + corr[a, b] for a in range(NV)], functools.partial(store, v), 4)
    fold_rim(pre, unpack("c4", "near"), near_slot)
    open_ring("c4", 0, True)
    far = unpack("c4", "far")
    for name, later in (("c4", "f5"), ("f5", "f6")):
        faces(functools.partial(swept_face, v, pre, cf, far), place_fine, later, full=later)
        open_ring(name, 1, True)
        sweep(v, pre, cf, far)
        send_others(later, v, place_fine)
        if later == "f6":
            save_v = pltpu.make_async_copy(v, r["v_out"], r["load_sem"].at[7])
            save_v.start()
        own(v, rhs, pre, 3.0 * WEIGHT, timed_fine)
        far = arrive(later, pre)
    open_ring("f6", 1, True)

    def last(b):
        at = rank[b]
        return rim([pre[a, b] - late[a, at] for a in range(NV)], b, far, far_slot)

    grouped(BD, last, functools.partial(store, pre), 4)
    save_r = pltpu.make_async_copy(pre, r["r_out"], r["load_sem"].at[8])
    save_r.start()
    for key in sem_index:
        if key[1] == "far":

            @pl.when(has_far)
            def _(key=key):
                copy_of(*key).wait_send()

        else:
            copy_of(*key).wait_send()
    save_v.wait()
    save_r.wait()


def finish(*refs):
    ins, outs, bufs, sems = refs[:2], refs[2:4], refs[4:6], refs[6]
    parts = []
    for i in range(2):
        for a in range(NV):
            parts.append(
                (
                    pltpu.make_async_copy(ins[i].at[a], bufs[i].at[a], sems.at[0, i, a]),
                    pltpu.make_async_copy(bufs[i].at[a], outs[i].at[a], sems.at[1, i, a]),
                )
            )
    for get, _ in parts:
        get.start()
    for get, put in parts:
        get.wait()
        put.start()
    for _, put in parts:
        put.wait()


def body(n_tm, n_space, iterate, right_side, jacobian, self_block, cell_diag, neighbours, face_list):
    def tiles(x):
        return x.reshape(T, NV, BD, BLK).transpose(1, 2, 0, 3)

    def untile(x):
        return x.transpose(2, 0, 1, 3).reshape(T, NV, BD * BLK)

    args = {
        "nb_in": neighbours.T,
        "fl_in": face_list,
        "v_in": tiles(iterate),
        "jac_in": jacobian.reshape(K, NV, NV, BD, BLK).transpose(1, 2, 3, 0, 4),
        "rhs_in": tiles(right_side),
        "sb_in": self_block.reshape(NV, NV, BD, BLK).transpose(0, 2, 1, 3),
        "dg_in": cell_diag.reshape(NV, BD, BLK).transpose(1, 0, 2),
    }
    field = (NV, BD, T, BLK)
    face = (NV, H, T, BLK)
    small = (NV, H // 4, T, BLK)
    scratch = {
        "v": field,
        "jac": (NV, NV, BD, K, BLK),
        "rhs": field,
        "sb": (NV, BD, NV, BLK),
        "dg": (BD, NV, BLK),
        "pre": field,
        "cf": field,
        "cc": field,
        "corr": field,
        "cpre": field,
        "cd": field,
        "late": field,
        "face_kept": face,
        "rim_near": face,
        "rim_far": face,
    }
    for name in FINE + SMALL:
        for key in ("face_out_", "near_in_", "far_in_"):
            scratch[key + name] = face if name in FINE else small
    for name in RING:
        for key in ("ring_out_", "ring_in_"):
            for part in ("_0", "_1"):
                scratch[key + name + part] = small
    n_sems = 2 * len(FINE + SMALL) + len(PARTS) - 1 + 2 * len(RING)
    names = list(args) + ["v_out", "r_out"] + list(scratch) + ["fl", "nb", "rank", "others", "load_sem", "send_sem", "recv_sem"]
    hbm = pl.BlockSpec(memory_space=pltpu.HBM)
    out = pl.pallas_call(
        functools.partial(kernel, n_tm, n_space, names),
        out_shape=(jax.ShapeDtypeStruct(field, jnp.float32),) * 2,
        in_specs=[hbm] * 7,
        out_specs=(hbm, hbm),
        scratch_shapes=[pltpu.VMEM(shape, jnp.float32) for shape in scratch.values()]
        + [
            pltpu.SMEM((H,), jnp.int32),
            pltpu.SMEM((K, BD), jnp.int32),
            pltpu.SMEM((BD,), jnp.int32),
            pltpu.SMEM((H,), jnp.int32),
            pltpu.SemaphoreType.DMA((9,)),
            pltpu.SemaphoreType.DMA((n_sems,)),
            pltpu.SemaphoreType.DMA((n_sems,)),
        ],
        compiler_params=pltpu.CompilerParams(
            collective_id=0, has_side_effects=True, vmem_limit_bytes=62 * 1024 * 1024
        ),
        name="vcycle",
    )(*args.values())
    out = pl.pallas_call(
        finish,
        out_shape=(jax.ShapeDtypeStruct(field, jnp.float32),) * 2,
        in_specs=[hbm] * 2,
        out_specs=(hbm, hbm),
        scratch_shapes=[pltpu.VMEM(field, jnp.float32)] * 2 + [pltpu.SemaphoreType.DMA((2, 2, NV))],
        compiler_params=pltpu.CompilerParams(vmem_limit_bytes=62 * 1024 * 1024),
        name="finish",
    )(*out)
    return tuple(untile(x) for x in out)


def solution(mesh):
    in_specs = (
        P("tm", None, "space"),
        P("tm", None, "space"),
        P(None, None, None, "space"),
        P(None, None, "space"),
        P(None, "space"),
        P("space", None),
        P("space"),
    )
    out_specs = (P("tm", None, "space"), P("tm", None, "space"))
    step = functools.partial(body, mesh.shape["tm"], mesh.shape["space"])
    return jax.shard_map(step, mesh=mesh, in_specs=in_specs, out_specs=out_specs, check_vma=False)
```

time: 75 us -> 68.4 us (0.912)
  the two profiles are of different devices: /device:TPU:73 before, /device:TPU:41 now
where the time goes in v1:
time: 68.4 us; the launch traced here: 67.9 us
  Pallas kernels  67.3 us (98%)
    pallas_call x1, Pallas kernels, body(): pl.pallas_call(functools.partial(kernel, n_tm, n_space, names), out_shape...  65.3 us
    pallas_call x1, Pallas kernels, body(): pl.pallas_call(finish, out_shape=(jax.ShapeDtypeStruct(field, jnp.float32...  1.92 us

profile of v1, /device:TPU:41, one launch (start us, length us, event | category | flops | bytes accessed | tf_op | source)
XLA Modules:
  0.0 67.9 jit_solution(11819224868413921043)
XLA Ops:
  0.6 65.3 %vcycle.1 = (f32[5,16,8,128]{3,2,1,0:T(8,128)}, f32[5,16,8,128]{3,2,1,0:T(8,128)}) custom-call(s32[6,16]{1,0:T(8,128)} %bitcast.27, s32[8]{0:T(128)} %refs_1_.1, f32[5,16,8,128]{3,2,1,0:T(8,128)} %bitcast.23, f32[5,5,16,6,128]{4,3,2,1,0:T(8,128)} %bitcast.22, f32[5,16,8,128]{3,2,1,0:T(8,128)} %bitcast.24, f32[5,16,5,128]{3,2,1,0:T(8,128)} %bitcast.25, ...), custom_call_target="tpu_custom_call" | custom-call | tf_op jit(solution)/shard_map/vcycle/pallas_call | solution.py:513
  66.0 1.9 %finish.1 = (f32[5,16,8,128]{3,2,1,0:T(8,128)}, f32[5,16,8,128]{3,2,1,0:T(8,128)}) custom-call(f32[5,16,8,128]{3,2,1,0:T(8,128)} %get-tuple-element.6.refs_0_, f32[5,16,8,128]{3,2,1,0:T(8,128)} %get-tuple-element.7.refs_1_), custom_call_target="tpu_custom_call" | custom-call | tf_op jit(solution)/shard_map/finish/pallas_call | solution.py:533

commit v2 on v1

--- a/solution.py
+++ b/solution.py
@@ -48,6 +48,7 @@
     cf, cc = r["cf"], r["cc"]
     corr, cpre, cd = r["corr"], r["cpre"], r["cd"]
     late, rank, others = r["late"], r["rank"], r["others"]
+    base, aim, jf, jc = r["base"], r["aim"], r["jf"], r["jc"]
 
     sub = lax.broadcasted_iota(jnp.int32, (T, BLK), 0)
     sub4 = lax.rem(sub, 4)
@@ -280,10 +281,30 @@
                 r["ring_out_" + ring_name + "_0"][a, g] = ring_tile(four, place)
         copy_of(ring_name, "ring0").start()
 
-    def swept_face(field, p, scale, far, h):
-        b = fl[h]
-        acc = rim([p[a, b] - late[a, h] for a in range(NV)], b, far, far_slot)
-        return [field[a, b] + scale[a, b] * acc[a] for a in range(NV)]
+    def prepare(values_of):
+        def step(g, carry):
+            at = [2 * g, 2 * g + 1]
+            got = [values_of(h, fl[h]) for h in at]
+            for h, values in zip(at, got):
+                store(base, h, values)
+            return carry
+
+        lax.fori_loop(0, H // 2, step, 0)
+
+    def prepare_sweep(field, p, scale):
+        def values_of(h, b):
+            return [field[a, b] + scale[a, b] * (p[a, b] - late[a, h]) for a in range(NV)]
+
+        prepare(values_of)
+
+    def face_value(table, far, h):
+        at = aim[h]
+        p = [far[j, at] for j in range(NV)]
+        values = []
+        for a in range(NV):
+            q = [table[h, NV * a + j] * p[j] for j in range(NV)]
+            values.append(base[a, h] - ((q[0] + q[1]) + (q[2] + q[3]) + q[4]))
+        return values
 
     def swept(field, p, scale, far, b):
         at = rank[b]
@@ -341,22 +362,36 @@
 
     grouped(BD, scales, keep_scales, 2)
 
+    def scaled(h, carry):
+        b = fl[h]
+        aim[h] = jnp.bitwise_and(nb[far_slot, b], H - 1)
+        for a in range(NV):
+            fine, coarse = cf[a, b], cc[a, b]
+            x = [row(jac, (a, j, b), far_slot) for j in range(NV)]
+            for j in range(NV):
+                jf[h, NV * a + j] = fine * x[j]
+                jc[h, NV * a + j] = coarse * x[j]
+        return carry
+
+    lax.fori_loop(0, H, scaled, 0)
+
     def arrive(name, out):
         wait(name, "near")
         fold_rim(out, r["near_in_" + name], near_slot)
         open_ring(name, 0, True)
+        prepare_sweep(v, out, cf)
         wait(name, "far")
         return r["far_in_" + name]
 
     own(v, rhs, pre, 3.0 * WEIGHT, timed_fine)
     far = arrive("f1", pre)
-    faces(functools.partial(swept_face, v, pre, cf, far), place_fine, "f2", full="f2")
+    faces(functools.partial(face_value, jf, far), place_fine, "f2", full="f2")
     open_ring("f1", 1, True)
     sweep(v, pre, cf, far)
     send_others("f2", v, place_fine)
     own(v, rhs, pre, 3.0 * WEIGHT, timed_fine)
     far = arrive("f2", pre)
-    faces(functools.partial(swept_face, v, pre, cf, far), place_fine, "f3", full="f3", small="c0", average=True)
+    faces(functools.partial(face_value, jf, far), place_fine, "f3", full="f3", small="c0", average=True)
     open_ring("f2", 1, True)
     sweep(v, pre, cf, far)
     send_others("f3", v, place_fine)
@@ -367,12 +402,8 @@
     grouped(BD, lambda b: [mean4(pre[a, b]) for a in range(NV)], functools.partial(store, cpre), 2)
     fold_rim(cpre, unpack("c0", "near"), near_slot)
     open_ring("f3", 0, True)
+    prepare(lambda h, b: [cc[a, b] * (cpre[a, b] - mean4(late[a, h])) for a in range(NV)])
     far = unpack("c0", "far")
-
-    def first_face(h):
-        b = fl[h]
-        acc = rim([cpre[a, b] - mean4(late[a, h]) for a in range(NV)], b, far, far_slot)
-        return [cc[a, b] * acc[a] for a in range(NV)]
 
     def first(b):
         q = [late[a, rank[b]] for a in range(NV)]
@@ -384,7 +415,7 @@
         store(corr, b, values[NV : 2 * NV])
         store(pre, b, values[2 * NV :])
 
-    faces(first_face, place_coarse, "c1", small="c1")
+    faces(functools.partial(face_value, jc, far), place_coarse, "c1", small="c1")
     open_ring("f3", 1, True)
     grouped(BD, first, keep_first, 2)
     send_others("c1", corr, place_coarse)
@@ -399,8 +430,9 @@
             for side, slot in (("near", near_slot), ("far", far_slot)):
                 wait("f3", side)
                 fold_rim(pre, r[side + "_in_f3"], slot)
+        prepare_sweep(corr, cpre, cc)
         far = unpack(name, "far")
-        faces(functools.partial(swept_face, corr, cpre, cc, far), place, later, small=later)
+        faces(functools.partial(face_value, jc, far), place, later, small=later)
         open_ring(name, 1, False)
         sweep(corr, cpre, cc, far)
         send_others(later, corr, place)
@@ -411,9 +443,10 @@
     grouped(BD, lambda b: [v[a, b] + corr[a, b] for a in range(NV)], functools.partial(store, v), 4)
     fold_rim(pre, unpack("c4", "near"), near_slot)
     open_ring("c4", 0, True)
+    prepare_sweep(v, pre, cf)
     far = unpack("c4", "far")
     for name, later in (("c4", "f5"), ("f5", "f6")):
-        faces(functools.partial(swept_face, v, pre, cf, far), place_fine, later, full=later)
+        faces(functools.partial(face_value, jf, far), place_fine, later, full=later)
         open_ring(name, 1, True)
         sweep(v, pre, cf, far)
         send_others(later, v, place_fine)
@@ -421,16 +454,30 @@
             save_v = pltpu.make_async_copy(v, r["v_out"], r["load_sem"].at[7])
             save_v.start()
         own(v, rhs, pre, 3.0 * WEIGHT, timed_fine)
-        far = arrive(later, pre)
+        if later == "f5":
+            far = arrive(later, pre)
+    wait("f6", "near")
+    fold_rim(pre, r["near_in_f6"], near_slot)
+    open_ring("f6", 0, True)
     open_ring("f6", 1, True)
-
-    def last(b):
-        at = rank[b]
-        return rim([pre[a, b] - late[a, at] for a in range(NV)], b, far, far_slot)
-
-    grouped(BD, last, functools.partial(store, pre), 4)
-    save_r = pltpu.make_async_copy(pre, r["r_out"], r["load_sem"].at[8])
-    save_r.start()
+    grouped(
+        BD,
+        lambda b: [pre[a, b] - late[a, rank[b]] for a in range(NV)],
+        functools.partial(store, pre),
+        4,
+    )
+    wait("f6", "far")
+    save_r = []
+    for g in range(4):
+        at = [4 * g + i for i in range(4)]
+        got = [rim([pre[a, b] for a in range(NV)], b, r["far_in_f6"], far_slot) for b in at]
+        for b, values in zip(at, got):
+            store(pre, b, values)
+        quarter = (slice(None), pl.ds(4 * g, 4))
+        save_r.append(
+            pltpu.make_async_copy(pre.at[quarter], r["r_out"].at[quarter], r["load_sem"].at[8 + g])
+        )
+        save_r[-1].start()
     for key in sem_index:
         if key[1] == "far":
 
@@ -441,7 +488,8 @@
         else:
             copy_of(*key).wait_send()
     save_v.wait()
-    save_r.wait()
+    for save in save_r:
+        save.wait()
 
 
 def finish(*refs):
@@ -497,6 +545,9 @@
         "cd": field,
         "late": field,
         "face_kept": face,
+        "base": face,
+        "jf": (H, NV * NV, T, BLK),
+        "jc": (H, NV * NV, T, BLK),
         "rim_near": face,
         "rim_far": face,
     }
@@ -508,7 +559,7 @@
             for part in ("_0", "_1"):
                 scratch[key + name + part] = small
     n_sems = 2 * len(FINE + SMALL) + len(PARTS) - 1 + 2 * len(RING)
-    names = list(args) + ["v_out", "r_out"] + list(scratch) + ["fl", "nb", "rank", "others", "load_sem", "send_sem", "recv_sem"]
+    names = list(args) + ["v_out", "r_out"] + list(scratch) + ["fl", "nb", "aim", "rank", "others", "load_sem", "send_sem", "recv_sem"]
     hbm = pl.BlockSpec(memory_space=pltpu.HBM)
     out = pl.pallas_call(
         functools.partial(kernel, n_tm, n_space, names),
@@ -519,9 +570,10 @@
         + [
             pltpu.SMEM((H,), jnp.int32),
             pltpu.SMEM((K, BD), jnp.int32),
+            pltpu.SMEM((H,), jnp.int32),
             pltpu.SMEM((BD,), jnp.int32),
             pltpu.SMEM((H,), jnp.int32),
-            pltpu.SemaphoreType.DMA((9,)),
+            pltpu.SemaphoreType.DMA((12,)),
             pltpu.SemaphoreType.DMA((n_sems,)),
             pltpu.SemaphoreType.DMA((n_sems,)),
         ],

time: 68.4 us -> 65.4 us (0.956)
  the two profiles are of different devices: /device:TPU:41 before, /device:TPU:120 now
where the time goes in v2:
time: 65.4 us; the launch traced here: 65.3 us
  Pallas kernels  64.6 us (99%)
    pallas_call x1, Pallas kernels, body(): pl.pallas_call(functools.partial(kernel, n_tm, n_space, names), out_shape...  62.7 us
    pallas_call x1, Pallas kernels, body(): pl.pallas_call(finish, out_shape=(jax.ShapeDtypeStruct(field, jnp.float32...  1.92 us

profile of v2, /device:TPU:120, one launch (start us, length us, event | category | flops | bytes accessed | tf_op | source)
XLA Modules:
  0.0 65.3 jit_solution(16935570860259539777)
XLA Ops:
  0.6 62.7 %vcycle.1 = (f32[5,16,8,128]{3,2,1,0:T(8,128)}, f32[5,16,8,128]{3,2,1,0:T(8,128)}) custom-call(s32[6,16]{1,0:T(8,128)} %bitcast.27, s32[8]{0:T(128)} %refs_1_.1, f32[5,16,8,128]{3,2,1,0:T(8,128)} %bitcast.23, f32[5,5,16,6,128]{4,3,2,1,0:T(8,128)} %bitcast.22, f32[5,16,8,128]{3,2,1,0:T(8,128)} %bitcast.24, f32[5,16,5,128]{3,2,1,0:T(8,128)} %bitcast.25, ...), custom_call_target="tpu_custom_call" | custom-call | tf_op jit(solution)/shard_map/vcycle/pallas_call | solution.py:564
  63.3 1.9 %finish.1 = (f32[5,16,8,128]{3,2,1,0:T(8,128)}, f32[5,16,8,128]{3,2,1,0:T(8,128)}) custom-call(f32[5,16,8,128]{3,2,1,0:T(8,128)} %get-tuple-element.6.refs_0_, f32[5,16,8,128]{3,2,1,0:T(8,128)} %get-tuple-element.7.refs_1_), custom_call_target="tpu_custom_call" | custom-call | tf_op jit(solution)/shard_map/finish/pallas_call | solution.py:585

commit v3 on v2

--- a/solution.py
+++ b/solution.py
@@ -493,23 +493,16 @@
 
 
 def finish(*refs):
-    ins, outs, bufs, sems = refs[:2], refs[2:4], refs[4:6], refs[6]
-    parts = []
-    for i in range(2):
-        for a in range(NV):
-            parts.append(
-                (
-                    pltpu.make_async_copy(ins[i].at[a], bufs[i].at[a], sems.at[0, i, a]),
-                    pltpu.make_async_copy(bufs[i].at[a], outs[i].at[a], sems.at[1, i, a]),
-                )
-            )
-    for get, _ in parts:
-        get.start()
-    for get, put in parts:
-        get.wait()
-        put.start()
-    for _, put in parts:
-        put.wait()
+    ins, outs, sems = refs[:2], refs[2:4], refs[4]
+    parts = [
+        pltpu.make_async_copy(ins[i].at[a], outs[i].at[a], sems.at[i, a])
+        for i in range(2)
+        for a in range(NV)
+    ]
+    for part in parts:
+        part.start()
+    for part in parts:
+        part.wait()
 
 
 def body(n_tm, n_space, iterate, right_side, jacobian, self_block, cell_diag, neighbours, face_list):
@@ -578,17 +571,17 @@
             pltpu.SemaphoreType.DMA((n_sems,)),
         ],
         compiler_params=pltpu.CompilerParams(
-            collective_id=0, has_side_effects=True, vmem_limit_bytes=62 * 1024 * 1024
+            collective_id=0, has_side_effects=True, vmem_limit_bytes=44 * 1024 * 1024
         ),
         name="vcycle",
-    )(*args.values())
+    )(*[pltpu.with_memory_space_constraint(x, pltpu.HBM) for x in args.values()])
     out = pl.pallas_call(
         finish,
-        out_shape=(jax.ShapeDtypeStruct(field, jnp.float32),) * 2,
-        in_specs=[hbm] * 2,
+        out_shape=(pltpu.HBM(field, jnp.float32),) * 2,
+        in_specs=[pl.BlockSpec(memory_space=pl.ANY)] * 2,
         out_specs=(hbm, hbm),
-        scratch_shapes=[pltpu.VMEM(field, jnp.float32)] * 2 + [pltpu.SemaphoreType.DMA((2, 2, NV))],
-        compiler_params=pltpu.CompilerParams(vmem_limit_bytes=62 * 1024 * 1024),
+        scratch_shapes=[pltpu.SemaphoreType.DMA((2, NV))],
+        compiler_params=pltpu.CompilerParams(vmem_limit_bytes=44 * 1024 * 1024),
         name="finish",
     )(*out)
     return tuple(untile(x) for x in out)

time: 65.4 us -> 63.9 us (0.977)
  Pallas kernels: 64.6 us -> 63.2 us
    pallas_call x1, Pallas kernels: 1.92 us -> 0.91 us  [body(): pl.pallas_call(finish, out_shape=(pltpu.HBM(field, jnp.float32),) * 2, in...]
where the time goes in v3:
time: 63.9 us; the launch traced here: 63.8 us
  Pallas kernels  63.2 us (99%)
  between operations  0.64 us (1%)
    pallas_call x1, Pallas kernels, body(): pl.pallas_call(functools.partial(kernel, n_tm, n_space, names), out_shape...  62.3 us

profile of v3, /device:TPU:120, one launch (start us, length us, event | category | flops | bytes accessed | tf_op | source)
XLA Modules:
  0.0 63.8 jit_solution(227256299156280002)
XLA Ops:
  0.6 62.3 %vcycle.1 = (f32[5,16,8,128]{3,2,1,0:T(8,128)S(1)}, f32[5,16,8,128]{3,2,1,0:T(8,128)S(1)}) custom-call(s32[6,16]{1,0:T(8,128)} %bitcast.27, s32[8]{0:T(128)} %refs_1_.1, f32[5,16,8,128]{3,2,1,0:T(8,128)} %bitcast.23, f32[5,5,16,6,128]{4,3,2,1,0:T(8,128)} %bitcast.22, f32[5,16,8,128]{3,2,1,0:T(8,128)} %bitcast.24, f32[5,16,5,128]{3,2,1,0:T(8,128)} %bitcast.25, ...), custom_call_target="tpu_custom_call" | custom-call | tf_op jit(solution)/shard_map/vcycle/pallas_call | solution.py:557
  62.9 0.9 %finish.1 = (f32[5,16,8,128]{3,2,1,0:T(8,128)}, f32[5,16,8,128]{3,2,1,0:T(8,128)}) custom-call(f32[5,16,8,128]{3,2,1,0:T(8,128)S(1)} %get-tuple-element.6.refs_0_, f32[5,16,8,128]{3,2,1,0:T(8,128)S(1)} %get-tuple-element.7.refs_1_), custom_call_target="tpu_custom_call" | custom-call | tf_op jit(solution)/shard_map/finish/pallas_call | solution.py:578

commit v4 on v3

--- a/solution.py
+++ b/solution.py
@@ -274,12 +274,15 @@
                     for i in range(1, 4):
                         tile = jnp.where(sub4 == i, four[i], tile)
                     r["face_out_" + small][a, g] = tile
-        send_faces(small or full)
+        if not small:
+            send_faces(full)
         for g in range(2):
             for a in range(NV):
                 four = [kept[a, 4 * g + i] for i in range(4)]
                 r["ring_out_" + ring_name + "_0"][a, g] = ring_tile(four, place)
         copy_of(ring_name, "ring0").start()
+        if small:
+            send_faces(small)
 
     def prepare(values_of):
         def step(g, carry):

time: 63.9 us -> 63.8 us (level)
  no operation moved by 1% of the time
where the time goes in v4:
time: 63.8 us; the launch traced here: 63.3 us
  Pallas kernels  62.6 us (98%)
  between operations  0.64 us (1%)
    pallas_call x1, Pallas kernels, body(): pl.pallas_call(functools.partial(kernel, n_tm, n_space, names), out_shape...  61.7 us

profile of v4, /device:TPU:120, one launch (start us, length us, event | category | flops | bytes accessed | tf_op | source)
XLA Modules:
  0.0 63.3 jit_solution(7285516616206320882)
XLA Ops:
  0.6 61.7 %vcycle.1 = (f32[5,16,8,128]{3,2,1,0:T(8,128)S(1)}, f32[5,16,8,128]{3,2,1,0:T(8,128)S(1)}) custom-call(s32[6,16]{1,0:T(8,128)} %bitcast.27, s32[8]{0:T(128)} %refs_1_.1, f32[5,16,8,128]{3,2,1,0:T(8,128)} %bitcast.23, f32[5,5,16,6,128]{4,3,2,1,0:T(8,128)} %bitcast.22, f32[5,16,8,128]{3,2,1,0:T(8,128)} %bitcast.24, f32[5,16,5,128]{3,2,1,0:T(8,128)} %bitcast.25, ...), custom_call_target="tpu_custom_call" | custom-call | tf_op jit(solution)/shard_map/vcycle/pallas_call | solution.py:560
  62.4 0.9 %finish.1 = (f32[5,16,8,128]{3,2,1,0:T(8,128)}, f32[5,16,8,128]{3,2,1,0:T(8,128)}) custom-call(f32[5,16,8,128]{3,2,1,0:T(8,128)S(1)} %get-tuple-element.6.refs_0_, f32[5,16,8,128]{3,2,1,0:T(8,128)S(1)} %get-tuple-element.7.refs_1_), custom_call_target="tpu_custom_call" | custom-call | tf_op jit(solution)/shard_map/finish/pallas_call | solution.py:581
